TPU v7x, 32 devices: a whole 2x2x4 slice. The times are simulated.
32 devices in a mesh: cell: 8 (over y, x, core), gene: 4 (over z).
Axes of the slice: x: 2, y: 2, z: 4, core: 2. Of those that a mesh axis runs over, the one named last changes fastest.
Arguments:
- counts: int32 [2048, 2560], P('cell', 'gene'), may hold values from 1 to 8
- cell_factors: float32 [64, 2048], P(None, 'cell'), may hold values from -6 to 6
- loadings: float32 [64, 2560], P(None, 'gene'), may hold values from -3 to 3
- cell_momenta: float32 [64, 2048], P(None, 'cell'), may hold values from -6 to 6
- loading_momenta: float32 [64, 2560], P(None, 'gene'), may hold values from -6 to 6
- step: float32 [64], replicated, may hold values from 0.01 to 0.04
Outputs:
- new_factors: float32 [64, 2048], P(None, 'cell')
- new_loadings: float32 [64, 2560], P(None, 'gene')
- new_cell_momenta: float32 [64, 2048], P(None, 'cell')
- new_loading_momenta: float32 [64, 2560], P(None, 'gene')
- log_rate: bfloat16 [2048, 2560], P('cell', 'gene')
All inputs are finite; a program needn't handle non-finite values.
Results may differ from a plain program's by a relative error of at most 0.001.
Values sent between devices are 32-bit elements; how exact they have to be, the bound alone decides.
No kernel may reach another device: no remote copies, remote signals or barrier semaphores. Data moves between devices by JAX's collectives and lax.ppermute only.
A program may use at most 64 MiB of HBM per device.

v0:
```python
import jax
import jax.numpy as jnp
from jax import lax
from jax.sharding import PartitionSpec as P

K = 64


def local(counts, cell_factors, loadings, cell_momenta, loading_momenta, step):
    scale = 1.0 / jnp.sqrt(jnp.float32(K))
    counts_float = counts.astype(jnp.float32)
    library = lax.psum(jnp.sum(counts_float, axis=1), "gene")
    genes_total = jnp.float32(loadings.shape[1] * lax.axis_size("gene"))
    half = 0.5 * step[:, None]
    full = step[:, None]
    width = loadings.shape[1] // lax.axis_size("cell")
    offset = lax.axis_index("cell") * width

    def gradient(factors, loads, own_loads):
        linear = (
            lax.dot_general(
                factors, loads, (((0,), (0,)), ((), ())), precision=lax.Precision.HIGHEST
            )
            * scale
        )
        expo = jnp.exp(linear)
        squares = jnp.sum(loads * loads, axis=1)
        total, squares = lax.psum((jnp.sum(expo, axis=1), squares), "gene")
        size = library / total
        resid = counts_float - size[:, None] * expo
        cross = (
            lax.dot_general(loads, resid, (((1,), (1,)), ((), ())), precision=lax.Precision.HIGHEST)
            * scale
        )
        grad_u = lax.psum(cross, "gene") - factors
        ard = (genes_total + 2.0) / (squares + 2.0)
        part_v = jnp.dot(factors, resid, precision=lax.Precision.HIGHEST) * scale
        grad_v = (
            lax.psum_scatter(part_v, "cell", scatter_dimension=1, tiled=True)
            - ard[:, None] * own_loads
        )
        return (grad_u, grad_v, linear, size)

    factors = cell_factors
    mom_u = cell_momenta
    loads = loadings
    own = lax.dynamic_slice_in_dim(loadings, offset, width, 1)
    mom_v = lax.dynamic_slice_in_dim(loading_momenta, offset, width, 1)
    grad_u, grad_v, linear, size = gradient(factors, loads, own)
    mom_u = mom_u + half * grad_u
    mom_v = mom_v + half * grad_v
    factors = factors + full * mom_u
    own = own + full * mom_v
    loads = lax.all_gather(own, "cell", axis=1, tiled=True)
    grad_u, grad_v, linear, size = gradient(factors, loads, own)
    mom_u = mom_u + half * grad_u
    mom_v = mom_v + half * grad_v
    mom_v = lax.all_gather(mom_v, "cell", axis=1, tiled=True)
    rates = (linear + jnp.log(size)[:, None]).astype(jnp.bfloat16)
    return (factors, loads, mom_u, mom_v, rates)


def solution(mesh):
    placed = (
        P("cell", "gene"),
        P(None, "cell"),
        P(None, "gene"),
        P(None, "cell"),
        P(None, "gene"),
        P(),
    )
    return jax.shard_map(
        local,
        mesh=mesh,
        in_specs=placed,
        out_specs=(
            P(None, "cell"),
            P(None, "gene"),
            P(None, "cell"),
            P(None, "gene"),
            P("cell", "gene"),
        ),
        check_vma=False,
    )
```

profile of v0, /device:TPU:0, one launch (start us, length us, event | category | flops | bytes accessed | tf_op | source)
XLA Modules:
  0.0 142.7 jit_solution(1274128571875531226)
XLA Ops:
  8.1 1.1 multiply_reduce_fusion.1
  9.2 1.3 convert_reduce_fusion
  10.5 0.9 fusion.5
  11.3 13.5 %all-reduce.1 = (f32[256]{0:T(256)S(1)}, f32[256]{0:T(256)S(1)}, f32[64]{0:T(128)S(1)}) all-reduce(f32[256]{0:T(256)S(1)} %convert_reduce_fusion, f32[256]{0:T(256)S(1)} %get-tuple-element.12, f32[64]{0:T(128)S(1)} %multiply_reduce_fusion.1), channel_id=1, replica_groups=mesh['cell'=8,'gene'=4] {'gene'}, use_global_device_ids=true, to_apply=%region_1.0 | all-reduce | flops 576 | bytes 4608 | tf_op jit(solution)/shard_map/psum | solution.py:12
  24.8 1.5 %fusion.2 = f32[64,256]{1,0:T(8,128)} fusion(f32[64,640]{1,0:T(8,128)S(1)} %copy-done.2, f32[256,640]{1,0:T(8,128)S(1)} %get-tuple-element.13, s32[256,640]{1,0:T(8,128)S(1)} %copy-done, f32[256]{0:T(256)S(1)} %div.12), kind=kOutput, calls=%fused_computation.8 | convolution fusion | flops 126337024 | bytes 1541120 | tf_op jit(solution)/shard_map/dot_general | solution.py:32
  27.0 0.9 copy.15
  28.6 30.4 %all-reduce.5.cloned.1.call-done = f32[64,256]{1,0:T(8,128)} async-done(((f32[64,256]{1,0:T(8,128)}), f32[64,256]{1,0:T(8,128)}) %all-reduce.5.cloned.1.call-update) | async-done | bytes 65552 | tf_op jit(solution)/shard_map/psum | solution.py:35
  59.0 0.9 multiply_add_fusion.1
  59.9 2.5 %reduce-scatter.7.cloned.1.call-done = f32[80,64]{1,0:T(8,128)} async-done(((f32[640,64]{1,0:T(8,128)}), f32[80,64]{1,0:T(8,128)}) %reduce-scatter.7.cloned.1.call-update) | async-done | bytes 20496
  62.5 0.8 copy.16
  63.3 1.0 fusion.3
  64.3 9.3 %all-gather = f32[8,80,64]{1,2,0:T(8,128)S(1)} all-gather(f32[1,80,64]{1,2,0:T(8,128)S(1)} %fusion.3), channel_id=1, replica_groups=mesh['cell'=8,'gene'=4] {'cell'}, dimensions={0}, use_global_device_ids=true | all-gather | bytes 184320 | tf_op jit(solution)/shard_map/all_gather | solution.py:54
  74.0 0.9 exponential_reduce_fusion
  74.8 11.7 %all-reduce = (f32[256]{0:T(256)S(1)}, f32[64]{0:T(128)S(1)}) all-reduce(f32[256]{0:T(256)S(1)} %get-tuple-element.14, f32[64]{0:T(128)S(1)} %multiply_reduce_fusion), channel_id=1, replica_groups=mesh['cell'=8,'gene'=4] {'gene'}, use_global_device_ids=true, to_apply=%region_9.0 | all-reduce | flops 320 | bytes 2560 | tf_op jit(solution)/shard_map/psum | solution.py:28
  86.5 1.5 %convolution_multiply_fusion.4 = f32[64,256]{1,0:T(8,128)} fusion(f32[640,64]{0,1:T(8,128)S(1)} %reshape.19, s32[256,640]{1,0:T(8,128)S(1)} %copy-done, f32[256,640]{1,0:T(8,128)S(1)} %get-tuple-element.15, f32[256]{0:T(256)S(1)} %get-tuple-element.11), kind=kOutput, calls=%fused_computation.6 | convolution fusion | flops 126337024 | bytes 1541120 | tf_op jit(solution)/shard_map/dot_general | solution.py:32
  88.7 0.8 add_convert_fusion
  89.5 0.9 copy.17
  90.5 29.9 %all-reduce.7.cloned.1.call-done = f32[64,256]{1,0:T(8,128)} async-done(((f32[64,256]{1,0:T(8,128)}), f32[64,256]{1,0:T(8,128)}) %all-reduce.7.cloned.1.call-update) | async-done | bytes 65552 | tf_op jit(solution)/shard_map/psum | solution.py:35
  120.3 1.5 %multiply_add_fusion = f32[64,256]{1,0:T(8,128)} fusion(f32[64,256]{1,0:T(8,128)} %all-reduce.7.cloned.1.call-done, f32[64,256]{1,0:T(8,128)S(1)} %multiply_add_fusion.1, f32[64]{0:T(128)S(1)} %broadcast_multiply_fusion, f32[64,256]{1,0:T(8,128)S(1)} %copy-done.5, f32[64,256]{1,0:T(8,128)S(1)} %copy-done.6, f32[64,256]{1,0:T(8,128)S(1)} %copy-done.3), kind=kLoop, calls=%fused_computation.16 | loop fusion | flops 98304 | bytes 393472 | tf_op jit(solution)/shard_map/add | solution.py:56
  121.9 1.4 reduce-scatter.9.cloned.1.call-done
  123.2 0.8 copy.18
  124.1 1.0 add_bitcast_fusion
  125.1 9.3 %all-gather.1 = f32[8,80,64]{1,2,0:T(8,128)S(1)} all-gather(f32[1,80,64]{1,2,0:T(8,128)S(1)} %add_bitcast_fusion), channel_id=1, replica_groups=mesh['cell'=8,'gene'=4] {'cell'}, dimensions={0}, use_global_device_ids=true | all-gather | bytes 184320 | tf_op jit(solution)/shard_map/all_gather | solution.py:58
  134.5 0.8 reshape.21
  (35 shorter events, 2.7 us)
Async XLA Ops:
  8.0 51.0 %all-reduce.5.cloned.1.call-start = ((), (), s32[]{:S(2)}) async-start(), calls=%async_computation.2 | async-start | bytes 131072 | tf_op jit(solution)/shard_map/psum | solution.py:35
  8.0 2.4 %copy-start.2 = (f32[64,640]{1,0:T(8,128)S(1)}, f32[64,640]{1,0:T(8,128)}, u32[]{:S(2)}) copy-start(f32[64,640]{1,0:T(8,128)} %param.8) | copy-start | bytes 491524
  8.1 2.4 %copy-start.3 = (f32[64,256]{1,0:T(8,128)S(1)}, f32[64,256]{1,0:T(8,128)}, u32[]{:S(2)}) copy-start(f32[64,256]{1,0:T(8,128)} %param.7) | copy-start | bytes 196612
  9.1 15.7 %copy-start = (s32[256,640]{1,0:T(8,128)S(1)}, s32[256,640]{1,0:T(8,128)}, u32[]{:S(2)}) copy-start(s32[256,640]{1,0:T(8,128)} %param.6) | copy-start | bytes 1966084
  26.3 36.1 %reduce-scatter.7.cloned.1.call-start = ((), (), s32[]{:S(2)}) async-start(), calls=%async_computation.4 | async-start | bytes 368640
  27.9 0.7 copy-start.7
  27.9 31.1 %copy-start.5 = (f32[64,256]{1,0:T(8,128)S(1)}, f32[64,256]{1,0:T(8,128)}, u32[]{:S(2)}) copy-start(f32[64,256]{1,0:T(8,128)} %param.9) | copy-start | bytes 196612
  27.9 92.4 %all-reduce.7.cloned.1.call-start = ((), (), s32[]{:S(2)}) async-start(), calls=%async_computation.3 | async-start | bytes 131072 | tf_op jit(solution)/shard_map/psum | solution.py:35
  59.9 60.4 %copy-start.4 = (f32[64,256]{1,0:T(8,128)}, f32[64,256]{1,0:T(8,128)S(1)}, u32[]{:S(2)}) copy-start(f32[64,256]{1,0:T(8,128)S(1)} %multiply_add_fusion.1) | copy-start | bytes 196612
  73.8 12.7 %copy-start.1 = (f32[640,64]{0,1:T(8,128)}, f32[640,64]{0,1:T(8,128)S(1)}, u32[]{:S(2)}) copy-start(f32[640,64]{0,1:T(8,128)S(1)} %reshape.19) | copy-start | bytes 491524
  88.7 34.6 %reduce-scatter.9.cloned.1.call-start = ((), (), s32[]{:S(2)}) async-start(), calls=%async_computation.5 | async-start | bytes 368640
  90.4 29.9 %copy-start.6 = (f32[64,256]{1,0:T(8,128)S(1)}, f32[64,256]{1,0:T(8,128)}, u32[]{:S(2)}) copy-start(f32[64,256]{1,0:T(8,128)} %all-reduce.5.cloned.1.call-done) | copy-start | bytes 196612
Sparse Core Ops, SparseCore 0:
  26.5 32.5 all-reduce.4
  88.8 31.5 all-reduce.6
Sparse Core Ops, SparseCore 1:
  30.4 32.0 reduce-scatter.6
  92.2 31.0 reduce-scatter.8
where the time goes:
time: 143 us
  waiting for transfers between devices  64.2 us (45%)
  blocking collectives  43.7 us (31%)
  between operations  15.6 us (11%)
  other arithmetic  7.73 us (5%)
  matrix products  5.94 us (4%)
  local copies, waits for them, and re-layouts  5.32 us (4%)
    psum x2, waiting for transfers between devices, gradient(): grad_u = lax.psum(cross, 'gene') - factors  60.3 us
    psum x1, blocking collectives, local(): library = lax.psum(jnp.sum(counts_float, axis=1), 'gene')  13.5 us
    psum x1, blocking collectives, gradient(): total, squares = lax.psum((jnp.sum(expo, axis=1), squares), 'gene')  11.7 us
    all_gather x1, blocking collectives, local(): loads = lax.all_gather(own, 'cell', axis=1, tiled=True)  9.26 us
    all_gather x1, blocking collectives, local(): mom_v = lax.all_gather(mom_v, 'cell', axis=1, tiled=True)  9.26 us
    unnamed x22, local copies, waits for them, and re-layouts  5.01 us
    unnamed x6, waiting for transfers between devices  3.93 us
    dot_general x2, matrix products, gradient(): lax.dot_general(loads, resid, (((1,), (1,)), ((), ())), precision=lax.Pre...  2.98 us
  transfers between devices with their start and end apart: 4, of which 4 were waited for; matrix products, arithmetic and copies ran while one was open for 4% of the time, Pallas kernels for 0%

commit v1 on v0

--- a/solution.py
+++ b/solution.py
@@ -32,7 +32,7 @@
             lax.dot_general(loads, resid, (((1,), (1,)), ((), ())), precision=lax.Precision.HIGHEST)
             * scale
         )
-        grad_u = lax.psum(cross, "gene") - factors
+        grad_u = jnp.sum(lax.all_gather(cross, "gene"), axis=0) - factors
         ard = (genes_total + 2.0) / (squares + 2.0)
         part_v = jnp.dot(factors, resid, precision=lax.Precision.HIGHEST) * scale
         grad_v = (

time: 143 us -> 149 us (1.042)
  blocking collectives: 43.7 us -> 71.3 us
  waiting for transfers between devices: 64.2 us -> 46.9 us
  other arithmetic: 7.73 us -> 4.95 us
    psum x2 -> x0, waiting for transfers between devices: 60.3 us -> none  [gradient(): grad_u = lax.psum(cross, 'gene') - factors]
    unnamed x6 -> x4, waiting for transfers between devices: 3.93 us -> 46.9 us
    all_gather x0 -> x2, blocking collectives: none -> 27.6 us  [gradient(): grad_u = jnp.sum(lax.all_gather(cross, 'gene'), axis=0) - factors]
    unnamed x22 -> x20, local copies, waits for them, and re-layouts: 5.01 us -> 5.25 us
  transfers between devices with their start and end apart: 4 -> 2, of which waited for: 4 -> 2; matrix products, arithmetic and copies ran while one was open for 4% -> 1% of each run, Pallas kernels for 0% -> 0%
where the time goes in v1:
time: 149 us
  blocking collectives  71.3 us (48%)
  waiting for transfers between devices  46.9 us (31%)
  between operations  14.2 us (10%)
  local copies, waits for them, and re-layouts  5.57 us (4%)
  matrix products  5.51 us (4%)
  other arithmetic  4.95 us (3%)
    unnamed x4, waiting for transfers between devices  46.9 us
    all_gather x2, blocking collectives, gradient(): grad_u = jnp.sum(lax.all_gather(cross, 'gene'), axis=0) - factors  27.6 us
    psum x1, blocking collectives, local(): library = lax.psum(jnp.sum(counts_float, axis=1), 'gene')  13.5 us
    psum x1, blocking collectives, gradient(): total, squares = lax.psum((jnp.sum(expo, axis=1), squares), 'gene')  11.7 us
    all_gather x1, blocking collectives, local(): mom_v = lax.all_gather(mom_v, 'cell', axis=1, tiled=True)  9.28 us
    all_gather x1, blocking collectives, local(): loads = lax.all_gather(own, 'cell', axis=1, tiled=True)  9.26 us
    unnamed x20, local copies, waits for them, and re-layouts  5.25 us
  transfers between devices with their start and end apart: 2, of which 2 were waited for; matrix products, arithmetic and copies ran while one was open for 1% of the time, Pallas kernels for 0%

profile of v1, /device:TPU:0, one launch (start us, length us, event | category | flops | bytes accessed | tf_op | source)
XLA Modules:
  0.0 148.6 jit_solution(15875680369450176986)
XLA Ops:
  7.2 1.1 multiply_reduce_fusion.1
  8.3 1.7 %fusion.5 = (f32[256]{0:T(256)S(1)}, f32[256,640]{1,0:T(8,128)S(1)}) fusion(f32[64,256]{1,0:T(8,128)} %param.7, f32[64,640]{1,0:T(8,128)S(1)} %copy-done.2), kind=kOutput, calls=%fused_computation.27 | convolution fusion | flops 126156544 | bytes 885760 | tf_op jit(solution)/shard_map/dot_general | solution.py:21
  10.2 13.5 %all-reduce.1 = (f32[256]{0:T(256)S(1)}, f32[256]{0:T(256)S(1)}, f32[64]{0:T(128)S(1)}) all-reduce(f32[256]{0:T(256)S(1)} %convert_reduce_fusion, f32[256]{0:T(256)S(1)} %get-tuple-element.12, f32[64]{0:T(128)S(1)} %multiply_reduce_fusion.1), channel_id=1, replica_groups=mesh['cell'=8,'gene'=4] {'gene'}, use_global_device_ids=true, to_apply=%region_1.0 | all-reduce | flops 576 | bytes 4608 | tf_op jit(solution)/shard_map/psum | solution.py:12
  23.7 0.6 fusion.1
  24.3 0.9 copy.15
  25.3 0.9 fusion.2
  26.2 13.8 %all-gather = f32[256,256]{1,0:T(8,128)S(1)} all-gather(f32[64,256]{1,0:T(8,128)S(1)} %fusion.2), channel_id=2, replica_groups=mesh['cell'=8,'gene'=4] {'gene'}, dimensions={0}, use_global_device_ids=true | all-gather | bytes 327680 | tf_op jit(solution)/shard_map/all_gather | solution.py:35
  40.0 0.8 copy-done.5
  41.0 16.4 %reduce-scatter.7.cloned.1.call-done = f32[80,64]{1,0:T(8,128)} async-done(((f32[640,64]{1,0:T(8,128)}), f32[80,64]{1,0:T(8,128)}) %reduce-scatter.7.cloned.1.call-update) | async-done | bytes 20496
  57.4 0.8 copy.16
  58.3 1.0 fusion.3
  59.2 9.3 %all-gather.2 = f32[8,80,64]{1,2,0:T(8,128)S(1)} all-gather(f32[1,80,64]{1,2,0:T(8,128)S(1)} %fusion.3), channel_id=1, replica_groups=mesh['cell'=8,'gene'=4] {'cell'}, dimensions={0}, use_global_device_ids=true | all-gather | bytes 184320 | tf_op jit(solution)/shard_map/all_gather | solution.py:54
  68.9 0.9 exponential_reduce_fusion
  69.8 11.7 %all-reduce = (f32[256]{0:T(256)S(1)}, f32[64]{0:T(128)S(1)}) all-reduce(f32[256]{0:T(256)S(1)} %get-tuple-element.14, f32[64]{0:T(128)S(1)} %multiply_reduce_fusion), channel_id=1, replica_groups=mesh['cell'=8,'gene'=4] {'gene'}, use_global_device_ids=true, to_apply=%region_9.0 | all-reduce | flops 320 | bytes 2560 | tf_op jit(solution)/shard_map/psum | solution.py:28
  81.5 0.8 convolution_multiply_fusion.4
  82.9 13.8 %all-gather.1 = f32[256,256]{1,0:T(8,128)S(1)} all-gather(f32[64,256]{1,0:T(8,128)S(1)} %convolution_multiply_fusion.4), channel_id=3, replica_groups=mesh['cell'=8,'gene'=4] {'gene'}, dimensions={0}, use_global_device_ids=true | all-gather | bytes 327680 | tf_op jit(solution)/shard_map/all_gather | solution.py:35
  96.8 0.7 multiply_add_fusion
  97.5 0.9 copy.17
  98.4 0.8 add_convert_fusion
  99.2 30.4 %reduce-scatter.9.cloned.1.call-done = f32[80,64]{1,0:T(8,128)} async-done(((f32[640,64]{1,0:T(8,128)}), f32[80,64]{1,0:T(8,128)}) %reduce-scatter.9.cloned.1.call-update) | async-done | bytes 20496
  129.7 0.8 copy.18
  130.5 1.0 add_bitcast_fusion
  131.5 9.3 %all-gather.3 = f32[8,80,64]{1,2,0:T(8,128)S(1)} all-gather(f32[1,80,64]{1,2,0:T(8,128)S(1)} %add_bitcast_fusion), channel_id=1, replica_groups=mesh['cell'=8,'gene'=4] {'cell'}, dimensions={0}, use_global_device_ids=true | all-gather | bytes 184320 | tf_op jit(solution)/shard_map/all_gather | solution.py:58
  140.9 0.8 reshape.23
  (31 shorter events, 1.6 us)
Async XLA Ops:
  7.2 1.2 copy-start.2
  7.2 2.9 %copy-start = (s32[256,640]{1,0:T(8,128)S(1)}, s32[256,640]{1,0:T(8,128)}, u32[]{:S(2)}) copy-start(s32[256,640]{1,0:T(8,128)} %param.6) | copy-start | bytes 1966084
  7.2 50.2 %reduce-scatter.7.cloned.1.call-start = ((), (), s32[]{:S(2)}) async-start(), calls=%async_computation.2 | async-start | bytes 368640
  10.0 13.6 %copy-start.3 = (f32[64,256]{1,0:T(8,128)S(1)}, f32[64,256]{1,0:T(8,128)}, u32[]{:S(2)}) copy-start(f32[64,256]{1,0:T(8,128)} %param.7) | copy-start | bytes 196612
  25.2 0.9 copy-start.6
  25.2 104.4 %reduce-scatter.9.cloned.1.call-start = ((), (), s32[]{:S(2)}) async-start(), calls=%async_computation.3 | async-start | bytes 368640
  40.0 0.8 copy-start.5
  41.0 55.8 %copy-start.4 = (f32[64,256]{1,0:T(8,128)}, f32[64,256]{1,0:T(8,128)S(1)}, u32[]{:S(2)}) copy-start(f32[64,256]{1,0:T(8,128)S(1)} %multiply_add_fusion.1) | copy-start | bytes 196612
  68.8 12.7 %copy-start.1 = (f32[640,64]{0,1:T(8,128)}, f32[640,64]{0,1:T(8,128)S(1)}, u32[]{:S(2)}) copy-start(f32[640,64]{0,1:T(8,128)S(1)} %reshape.21) | copy-start | bytes 491524
Sparse Core Ops, SparseCore 0:
  25.4 32.0 reduce-scatter.6
  98.5 31.0 reduce-scatter.8
